TPU v7x, 32 devices: a whole 2x2x4 slice. The times are simulated.
32 devices in a mesh: dp: 4 (over y, core), proto: 8 (over z, x).
Axes of the slice: x: 2, y: 2, z: 4, core: 2. Of those that a mesh axis runs over, the one named last changes fastest.
Arguments:
- student_rows: bfloat16 [64, 256, 256], P('dp'), may hold values from -0.375 to 0.375
- teacher_rows: bfloat16 [64, 256, 256], P('dp'), may hold values from -0.375 to 0.375
- student_proto: bfloat16 [256, 131072], P(None, 'proto'), may hold values from -0.375 to 0.375
- teacher_proto: bfloat16 [256, 131072], P(None, 'proto'), may hold values from -0.375 to 0.375
- center: float32 [131072], P('proto'), may hold values from -0.05 to 0.05
- counts: int32 [64], replicated, may hold values from 1 to 128, 6144 in all
- mask_order: int32 [64, 256], P('dp'), may hold values from 0 to 255, each once within a row
Outputs:
- row_loss: float32 [4, 1536], P('dp')
- student_grad: bfloat16 [4, 1536, 256], P('dp')
Inputs may be any that keep to these rules, and one draw needn't show every extreme that they name: counts sum to 6144, and some image has exactly 128. `mask_order`: each row is a permutation of the patch positions; image i's masked patches are its first counts[i] entries.
All inputs are finite; a program needn't handle non-finite values.
Results may differ from a plain program's by a relative error of at most 0.002.
The roundings to bfloat16 on the way count: a program that leaves them out, or rounds other values in their place, can miss the bound.
Values may be sent and summed in bfloat16 or wider, within the bound.
No kernel may reach another device: no remote copies, remote signals or barrier semaphores. Data moves between devices by JAX's collectives and lax.ppermute only.
A program may use at most 320 MiB of HBM per device.

v0:
```python
import jax
import jax.numpy as jnp
from jax import lax
from jax.sharding import PartitionSpec as P

MASK_IMG = 96
STUDENT_TEMP = 0.1
TEACHER_TEMP = 0.07
EPSILON = 1e-06


def norm_columns(weights):
    wide = weights.astype(jnp.float32)
    return (wide / jnp.sqrt(jnp.sum(wide * wide, axis=0, keepdims=True) + EPSILON)).astype(
        jnp.bfloat16
    )


def backward(student_in, student_norm, feature_grad):
    inner = jnp.sum(student_in * feature_grad, axis=-1, keepdims=True)
    return feature_grad / student_norm - student_in * inner / (
        student_norm * student_norm * student_norm
    )


def proto_head(student_part, teacher_part, student_cols, teacher_cols, center):
    student_in = student_part.astype(jnp.float32)
    teacher_in = teacher_part.astype(jnp.float32)
    student_norm = jnp.sqrt(jnp.sum(student_in * student_in, axis=-1, keepdims=True) + EPSILON)
    teacher_norm = jnp.sqrt(jnp.sum(teacher_in * teacher_in, axis=-1, keepdims=True) + EPSILON)
    student_unit = (student_in / student_norm).astype(jnp.bfloat16)
    teacher_unit = (teacher_in / teacher_norm).astype(jnp.bfloat16)
    student_logit = jnp.dot(student_unit, student_cols, preferred_element_type=jnp.float32)
    teacher_logit = jnp.dot(teacher_unit, teacher_cols, preferred_element_type=jnp.float32)
    student_exp = jnp.exp(student_logit / STUDENT_TEMP)
    teacher_exp = jnp.exp((teacher_logit - center[None, :]) / TEACHER_TEMP)
    totals = lax.psum(
        (
            jnp.sum(student_exp, axis=1),
            jnp.sum(teacher_exp, axis=1),
            jnp.sum(teacher_exp * (student_logit / STUDENT_TEMP), axis=1),
        ),
        "proto",
    )
    student_sum, teacher_sum, cross_sum = totals
    row_losses = jnp.log(student_sum) - cross_sum / teacher_sum
    logit_grad = (
        (student_exp / student_sum[:, None] - teacher_exp / teacher_sum[:, None]) / STUDENT_TEMP
    ).astype(jnp.bfloat16)
    feature_grad = lax.dot_general(
        logit_grad, student_cols, (((1,), (1,)), ((), ())), preferred_element_type=jnp.float32
    )
    feature_grad = lax.psum(feature_grad, "proto")
    input_grad = backward(student_in, student_norm, feature_grad)
    return (row_losses, input_grad)


def local(student_rows, teacher_rows, student_proto, teacher_proto, center, counts, mask_order):
    img_dev, patches, feature_width = student_rows.shape
    dp_count = lax.axis_size("dp")
    dp_index = lax.axis_index("dp")
    capacity = img_dev * (patches // 2)
    slot_count = (capacity + dp_count - 1) // dp_count
    mask_dev = MASK_IMG * img_dev
    dev_counts = jnp.sum(counts.reshape(dp_count, img_dev), axis=1)
    dev_ends = jnp.cumsum(dev_counts)
    dev_starts = dev_ends - dev_counts
    is_owner = jnp.arange(dp_count, dtype=jnp.int32) == dp_index
    own_start = jnp.sum(jnp.where(is_owner, dev_starts, 0))
    own_count = jnp.sum(jnp.where(is_owner, dev_counts, 0))
    local_counts = lax.dynamic_slice_in_dim(counts, dp_index * img_dev, img_dev)
    local_ends = jnp.cumsum(local_counts)
    local_starts = local_ends - local_counts
    order_flat = mask_order.reshape(-1)
    targets = jnp.arange(dp_count, dtype=jnp.int32)[:, None]
    slot_ids = jnp.arange(slot_count, dtype=jnp.int32)[None, :]
    send_pos = jnp.mod(targets - own_start, dp_count) + slot_ids * dp_count
    send_valid = send_pos < own_count
    balanced = jnp.arange(mask_dev, dtype=jnp.int32)
    global_pos = balanced * dp_count + dp_index
    source = jnp.sum((global_pos[:, None] >= dev_ends[None, :]).astype(jnp.int32), axis=1)
    source_start = jnp.take(dev_starts, source)
    first_pos = source_start + jnp.mod(dp_index - source_start, dp_count)
    receive_ids = source * slot_count + (global_pos - first_pos) // dp_count
    student_flat = student_rows.reshape(img_dev * patches, feature_width)
    teacher_flat = teacher_rows.reshape(img_dev * patches, feature_width)
    student_cols = norm_columns(student_proto)
    teacher_cols = norm_columns(teacher_proto)
    image_ids = jnp.minimum(
        jnp.sum((send_pos[..., None] >= local_ends).astype(jnp.int32), axis=-1), img_dev - 1
    )
    within = jnp.clip(send_pos - jnp.take(local_starts, image_ids), 0, patches - 1)
    patch_ids = jnp.take(order_flat, image_ids * patches + within)
    row_ids = image_ids * patches + patch_ids
    keep_mask = send_valid[..., None]
    send_student = jnp.where(keep_mask, jnp.take(student_flat, row_ids, axis=0), 0)
    send_teacher = jnp.where(keep_mask, jnp.take(teacher_flat, row_ids, axis=0), 0)
    got_student, got_teacher = (
        lax.all_to_all(send_student, "dp", split_axis=0, concat_axis=0, tiled=True),
        lax.all_to_all(send_teacher, "dp", split_axis=0, concat_axis=0, tiled=True),
    )
    student_part = jnp.take(
        got_student.reshape(dp_count * slot_count, feature_width), receive_ids, axis=0
    )
    teacher_part = jnp.take(
        got_teacher.reshape(dp_count * slot_count, feature_width), receive_ids, axis=0
    )
    row_losses, input_grad = proto_head(
        student_part, teacher_part, student_cols, teacher_cols, center
    )
    return (row_losses[None, :], input_grad.astype(jnp.bfloat16)[None])


def solution(mesh):
    placed = (
        P("dp", None, None),
        P("dp", None, None),
        P(None, "proto"),
        P(None, "proto"),
        P("proto"),
        P(),
        P("dp", None),
    )
    return jax.shard_map(
        local,
        mesh=mesh,
        in_specs=placed,
        out_specs=(P("dp", None), P("dp", None, None)),
        check_vma=False,
    )
```

profile of v0, /device:TPU:0, one launch (start us, length us, event | category | flops | bytes accessed | tf_op | source)
XLA Modules:
  0.0 418.9 jit_solution(7376634795189560316)
XLA Ops:
  7.2 0.9 reshape.344
  11.6 12.6 %gather_fusion = s32[2048]{0:T(1024)S(1)} fusion(s32[16]{0:T(128)S(1)} %dynamic-slice_subtract_fusion, s32[2048]{0:T(1024)S(1)} %broadcast_clamp_fusion.2), kind=kCustom, calls=%fused_computation.4 | custom fusion | bytes 24576 | tf_op jit(solution)/shard_map/jit(_take)/gather | solution.py:92
  24.4 11.8 %gather_fusion.1 = s32[2048]{0:T(1024)S(1)} fusion(s32[4096]{0:T(1024)S(1)} %bitcast.43, s32[2048]{0:T(1024)S(1)} %broadcast_clamp_fusion.1), kind=kCustom, calls=%fused_computation.5 | custom fusion | bytes 24576 | tf_op jit(solution)/shard_map/jit(_take)/gather | solution.py:93
  37.0 7.5 %gather_fusion.4 = bf16[2048,256]{1,0:T(8,128)(2,1)S(1)} fusion(bf16[4096,256]{1,0:T(8,128)(2,1)S(1)} %bitcast.42, s32[2048]{0:T(1024)S(1)} %broadcast_clamp_fusion), kind=kCustom, calls=%fused_computation.2.clone | custom fusion | bytes 2105344 | tf_op jit(solution)/shard_map/jit(_take)/gather | solution.py:97
  44.5 10.3 %gather_fusion.2 = bf16[2048,256]{1,0:T(8,128)(2,1)} fusion(bf16[4096,256]{1,0:T(8,128)(2,1)} %bitcast.45, s32[2048]{0:T(1024)S(1)} %broadcast_clamp_fusion), kind=kCustom, calls=%fused_computation.clone | custom fusion | bytes 2105344 | tf_op jit(solution)/shard_map/jit(_take)/gather | solution.py:96
  54.8 3.7 select_select_fusion
  58.5 4.3 %all-to-all-start = ((bf16[4,512,256]{2,1,0:T(8,128)(2,1)}), bf16[4,512,256]{2,1,0:T(8,128)(2,1)S(1)}, u32[]{:S(2)}, u32[]{:S(2)}) async-start(bf16[4,512,256]{2,1,0:T(8,128)(2,1)} %get-tuple-element.21), calls=%async_computation | async-start | bytes 2097152 | tf_op jit(solution)/shard_map/all_to_all | solution.py:99
  62.7 5.1 %fusion.3 = f32[16384]{0:T(1024)S(1)} fusion(bf16[256,16384]{1,0:T(8,128)(2,1)} %param.14), kind=kLoop, calls=%fused_computation.17 | loop fusion | flops 12566528 | bytes 8454144 | tf_op jit(solution)/shard_map/reduce_sum | solution.py:14
  68.6 2.5 fusion.31
  71.2 5.1 %fusion.1 = f32[16384]{0:T(1024)S(1)} fusion(bf16[256,16384]{1,0:T(8,128)(2,1)} %param.13), kind=kLoop, calls=%fused_computation.15 | loop fusion | flops 12566528 | bytes 8454144 | tf_op jit(solution)/shard_map/reduce_sum | solution.py:14
  76.3 0.9 all-to-all-done
  77.2 4.3 %all-to-all-start.1 = ((bf16[4,512,256]{2,1,0:T(8,128)(2,1)}), bf16[4,512,256]{2,1,0:T(8,128)(2,1)}, u32[]{:S(2)}, u32[]{:S(2)}) async-start(bf16[4,512,256]{2,1,0:T(8,128)(2,1)} %get-tuple-element.20), calls=%async_computation.1 | async-start | bytes 2097152 | tf_op jit(solution)/shard_map/all_to_all | solution.py:100
  81.7 5.4 %gather_fusion.3 = bf16[1536,256]{1,0:T(8,128)(2,1)} fusion(bf16[2048,256]{1,0:T(8,128)(2,1)S(1)} %bitcast.44, s32[2048]{0:T(1024)S(1)} %pad_clamp_fusion), kind=kCustom, calls=%fused_computation.1.clone | custom fusion | bytes 1579008 | tf_op jit(solution)/shard_map/jit(_take)/gather | solution.py:102
  87.1 8.8 %all-to-all-done.1 = bf16[4,512,256]{2,1,0:T(8,128)(2,1)} async-done(((bf16[4,512,256]{2,1,0:T(8,128)(2,1)}), bf16[4,512,256]{2,1,0:T(8,128)(2,1)}, u32[]{:S(2)}, u32[]{:S(2)}) %all-to-all-start.1) | async-done | bytes 1048608 | tf_op jit(solution)/shard_map/all_to_all | solution.py:100
  95.9 5.9 %gather_fusion.5 = bf16[1536,256]{1,0:T(8,128)(2,1)} fusion(bf16[2048,256]{1,0:T(8,128)(2,1)} %bitcast.13, s32[2048]{0:T(1024)S(1)} %pad_clamp_fusion), kind=kCustom, calls=%fused_computation.3.clone | custom fusion | bytes 1579008 | tf_op jit(solution)/shard_map/jit(_take)/gather | solution.py:105
  101.8 2.2 fusion.9
  104.6 1.8 fusion.16.clone.5
  106.4 39.1 %multiply_exponential_fusion = f32[1536,16384]{1,0:T(8,128)} fusion(f32[16384]{0:T(1024)S(1)} %copy-done.11, bf16[256,16384]{1,0:T(8,128)(2,1)} %param.14, f32[16384]{0:T(1024)S(1)} %add_sqrt_fusion, f32[1536]{0:T(1024)S(1)} %get-tuple-element.29, bf16[1536,256]{1,0:T(8,128)(2,1)} %gather_fusion.5, pred[1536]{0:T(1024)(128)(4,1)S(1)} %get-tuple-element.12), kind=kOutput, calls=%fused_computation.8 | convolution fusion | flops 12949389312 | bytes 109977088 | tf_op jit(solution)/shard_map/dot_general | solution.py:34
  145.4 70.0 %exponential_reduce_fusion = (f32[1536]{0:T(1024)S(1)}, f32[1536]{0:T(1024)S(1)}, f32[1536]{0:T(1024)S(1)}, f32[1536,16384]{1,0:T(8,128)}) fusion(f32[1536,16384]{1,0:T(8,128)} %multiply_exponential_fusion, bf16[256,16384]{1,0:T(8,128)(2,1)} %param.13, f32[16384]{0:T(1024)S(1)} %add_sqrt_fusion.1, bf16[1536,256]{1,0:T(8,128)(2,1)S(1)} %copy-done.3), kind=kOutput, calls=%fused_computation.9 | convolution fusion | flops 13023307776 | bytes 210585600 | tf_op jit(solution)/shard_map/dot_general | solution.py:33
  215.4 38.1 %all-reduce = (f32[1536]{0:T(1024)}, f32[1536]{0:T(1024)S(1)}, f32[1536]{0:T(1024)S(1)}) all-reduce(f32[1536]{0:T(1024)S(1)} %get-tuple-element.5, f32[1536]{0:T(1024)S(1)} %get-tuple-element.6, f32[1536]{0:T(1024)S(1)} %get-tuple-element.4), channel_id=1, replica_groups=mesh['dp'=4,'proto'=8] {'proto'}, use_global_device_ids=true, to_apply=%region_14.17 | all-reduce | flops 4608 | bytes 36864 | tf_op jit(solution)/shard_map/psum | solution.py:37
  253.6 67.1 %fusion = f32[1536,256]{1,0:T(8,128)} fusion(f32[1536,16384]{1,0:T(8,128)} %multiply_exponential_fusion, f32[1536,16384]{1,0:T(8,128)} %get-tuple-element.28, f32[1536]{0:T(1024)S(1)} %get-tuple-element.10, f32[1536]{0:T(1024)S(1)} %get-tuple-element.11, bf16[256,16384]{1,0:T(8,128)(2,1)} %param.13, f32[16384]{0:T(1024)S(1)} %add_sqrt_fusion.1), kind=kOutput, calls=%fused_computation.10 | convolution fusion | flops 13048479744 | bytes 211365888 | tf_op jit(solution)/shard_map/dot_general | solution.py:50
  321.4 84.9 %all-reduce.3.cloned.1.call-done = f32[1536,256]{1,0:T(8,128)} async-done(((f32[1536,256]{1,0:T(8,128)}), f32[1536,256]{1,0:T(8,128)}) %all-reduce.3.cloned.1.call-update) | async-done | bytes 1572880 | tf_op jit(solution)/shard_map/psum | solution.py:53
  406.3 1.9 fusion.11
  408.2 3.8 fusion.20
  (61 shorter events, 6.7 us)
Async XLA Ops:
  7.2 29.8 %copy-start = (bf16[16,256,256]{2,1,0:T(8,128)(2,1)S(1)}, bf16[16,256,256]{2,1,0:T(8,128)(2,1)}, u32[]{:S(2)}) copy-start(bf16[16,256,256]{2,1,0:T(8,128)(2,1)} %param.12) | copy-start | bytes 6291460
  7.2 17.1 %copy-start.9 = (s32[16,256]{1,0:T(8,128)S(1)}, s32[16,256]{1,0:T(8,128)}, u32[]{:S(2)}) copy-start(s32[16,256]{1,0:T(8,128)} %param.17) | copy-start | bytes 49156
  58.5 18.7 %all-to-all-start = ((bf16[4,512,256]{2,1,0:T(8,128)(2,1)}), bf16[4,512,256]{2,1,0:T(8,128)(2,1)S(1)}, u32[]{:S(2)}, u32[]{:S(2)}) async-start(bf16[4,512,256]{2,1,0:T(8,128)(2,1)} %get-tuple-element.21), calls=%async_computation | async-start | bytes 2097152 | tf_op jit(solution)/shard_map/all_to_all | solution.py:99
  71.1 35.2 %copy-start.6 = (pred[1536]{0:T(1024)(128)(4,1)}, pred[1536]{0:T(1024)(128)(4,1)S(1)}, u32[]{:S(2)}) copy-start(pred[1536]{0:T(1024)(128)(4,1)S(1)} %get-tuple-element.12) | copy-start | bytes 4612
  77.2 18.8 %all-to-all-start.1 = ((bf16[4,512,256]{2,1,0:T(8,128)(2,1)}), bf16[4,512,256]{2,1,0:T(8,128)(2,1)}, u32[]{:S(2)}, u32[]{:S(2)}) async-start(bf16[4,512,256]{2,1,0:T(8,128)(2,1)} %get-tuple-element.20), calls=%async_computation.1 | async-start | bytes 2097152 | tf_op jit(solution)/shard_map/all_to_all | solution.py:100
  81.4 324.9 %all-reduce.3.cloned.1.call-start = ((), (), s32[]{:S(2)}) async-start(), calls=%async_computation.2 | async-start | bytes 3145728 | tf_op jit(solution)/shard_map/psum | solution.py:53
  81.7 24.6 %copy-start.11 = (f32[16384]{0:T(1024)S(1)}, f32[16384]{0:T(1024)}, u32[]{:S(2)}) copy-start(f32[16384]{0:T(1024)} %param.15) | copy-start | bytes 196612
  87.1 17.5 %copy-start.1 = (bf16[1536,256]{1,0:T(8,128)(2,1)S(1)}, bf16[1536,256]{1,0:T(8,128)(2,1)}, u32[]{:S(2)}) copy-start(bf16[1536,256]{1,0:T(8,128)(2,1)} %gather_fusion.3) | copy-start | bytes 2359300
  104.6 1.8 copy-start.4
  106.4 39.1 %copy-start.3 = (bf16[1536,256]{1,0:T(8,128)(2,1)S(1)}, bf16[1536,256]{1,0:T(8,128)(2,1)}, u32[]{:S(2)}) copy-start(bf16[1536,256]{1,0:T(8,128)(2,1)} %fusion.16.clone.5) | copy-start | bytes 2359300
  253.5 67.2 %copy-start.10 = (f32[1536]{0:T(1024)S(1)}, f32[1536]{0:T(1024)}, u32[]{:S(2)}) copy-start(f32[1536]{0:T(1024)} %get-tuple-element.9) | copy-start | bytes 18436
  253.5 152.8 %copy-start.2 = (bf16[1536,256]{1,0:T(8,128)(2,1)S(1)}, bf16[1536,256]{1,0:T(8,128)(2,1)}, u32[]{:S(2)}) copy-start(bf16[1536,256]{1,0:T(8,128)(2,1)} %gather_fusion.3) | copy-start | bytes 2359300
  253.5 152.8 %copy-start.7 = (pred[1536]{0:T(1024)(128)(4,1)S(1)}, pred[1536]{0:T(1024)(128)(4,1)}, u32[]{:S(2)}) copy-start(pred[1536]{0:T(1024)(128)(4,1)} %copy-done.6) | copy-start | bytes 4612
  253.5 154.7 %copy-start.5 = (f32[1536]{0:T(1024)S(1)}, f32[1536]{0:T(1024)}, u32[]{:S(2)}) copy-start(f32[1536]{0:T(1024)} %copy-done.4) | copy-start | bytes 18436
  253.6 154.7 %copy-start.8 = (f32[1536]{0:T(1024)S(1)}, f32[1536]{0:T(1024)}, u32[]{:S(2)}) copy-start(f32[1536]{0:T(1024)} %get-tuple-element.18) | copy-start | bytes 18436
Sparse Core Ops, SparseCore 0:
  320.9 85.3 all-reduce.2
where the time goes:
time: 420 us; the launch traced here: 419 us
  matrix products  176 us (42%)
  waiting for transfers between devices  94.6 us (23%)
  local copies, waits for them, and re-layouts  56.4 us (13%)
  blocking collectives  38.1 us (9%)
  other arithmetic  30.5 us (7%)
  between operations  14.3 us (3%)
  starting transfers between devices  8.75 us (2%)
    psum x1, waiting for transfers between devices, proto_head(): feature_grad = lax.psum(feature_grad, 'proto')  84.9 us
    dot_general x1, matrix products, proto_head(): jnp.dot(student_unit, student_cols, preferred_element_type=jnp.float32)  70 us
    dot_general x1, matrix products, proto_head(): lax.dot_general(logit_grad, student_cols, (((1,), (1,)), ((), ())), prefe...  67.1 us
    dot_general x1, matrix products, proto_head(): jnp.dot(teacher_unit, teacher_cols, preferred_element_type=jnp.float32)  39.1 us
    psum x1, blocking collectives, proto_head(): lax.psum((jnp.sum(student_exp, axis=1), jnp.sum(teacher_exp, axis=1), jnp...  38.1 us
    gather x3, local copies, waits for them, and re-layouts, local(): jnp.take(local_starts, image_ids)  12.6 us
    gather x2, local copies, waits for them, and re-layouts, local(): patch_ids = jnp.take(order_flat, image_ids * patches + within)  11.8 us
    gather x1, local copies, waits for them, and re-layouts, local(): jnp.take(student_flat, row_ids, axis=0)  10.3 us
  transfers between devices with their start and end apart: 3, of which 3 were waited for; matrix products, arithmetic and copies ran while one was open for 5% of the time, Pallas kernels for 0%

commit v1 on v0

--- a/solution.py
+++ b/solution.py
@@ -50,7 +50,11 @@
     feature_grad = lax.dot_general(
         logit_grad, student_cols, (((1,), (1,)), ((), ())), preferred_element_type=jnp.float32
     )
-    feature_grad = lax.psum(feature_grad, "proto")
+    feature_grad = feature_grad
+    for hop in (1, 2, 4):
+        feature_grad = feature_grad + lax.ppermute(
+            feature_grad, "proto", [(dev, dev ^ hop) for dev in range(8)]
+        )
     input_grad = backward(student_in, student_norm, feature_grad)
     return (row_losses, input_grad)
 

time: 420 us -> 435 us (1.036)
  waiting for transfers between devices: 94.6 us -> 125 us
  between operations: 14.3 us -> 0.97 us
  other arithmetic: 30.5 us -> 25.4 us
    ppermute x0 -> x3, waiting for transfers between devices: none -> 117 us  [proto_head(): lax.ppermute(feature_grad, 'proto', [(dev, dev ^ hop) for dev in range(8)])]
    psum x1 -> x0, waiting for transfers between devices: 84.9 us -> none  [proto_head(): feature_grad = lax.psum(feature_grad, 'proto')]
    all_to_all x1, waiting for transfers between devices: 8.82 us -> 0.83 us  [local(): lax.all_to_all(send_teacher, 'dp', split_axis=0, concat_axis=0, tiled=True)]
    all_to_all x1, waiting for transfers between devices: 0.87 us -> 7.24 us  [local(): lax.all_to_all(send_student, 'dp', split_axis=0, concat_axis=0, tiled=True)]
  transfers between devices with their start and end apart: 3 -> 5, of which waited for: 3 -> 5; matrix products, arithmetic and copies ran while one was open for 5% -> 5% of each run, Pallas kernels for 0% -> 0%
where the time goes in v1:
time: 435 us; the launch traced here: 434 us
  matrix products  176 us (40%)
  waiting for transfers between devices  125 us (29%)
  local copies, waits for them, and re-layouts  59 us (14%)
  blocking collectives  38.1 us (9%)
  other arithmetic  25.4 us (6%)
  starting transfers between devices  8.92 us (2%)
    ppermute x3, waiting for transfers between devices, proto_head(): lax.ppermute(feature_grad, 'proto', [(dev, dev ^ hop) for dev in range(8)])  117 us
    dot_general x1, matrix products, proto_head(): jnp.dot(student_unit, student_cols, preferred_element_type=jnp.float32)  69.8 us
    dot_general x1, matrix products, proto_head(): lax.dot_general(logit_grad, student_cols, (((1,), (1,)), ((), ())), prefe...  67.5 us
    dot_general x1, matrix products, proto_head(): jnp.dot(teacher_unit, teacher_cols, preferred_element_type=jnp.float32)  39 us
    psum x1, blocking collectives, proto_head(): lax.psum((jnp.sum(student_exp, axis=1), jnp.sum(teacher_exp, axis=1), jnp...  38.1 us
    gather x3, local copies, waits for them, and re-layouts, local(): jnp.take(local_starts, image_ids)  12.6 us
    gather x2, local copies, waits for them, and re-layouts, local(): patch_ids = jnp.take(order_flat, image_ids * patches + within)  11.8 us
    gather x1, local copies, waits for them, and re-layouts, local(): jnp.take(student_flat, row_ids, axis=0)  10.3 us
  transfers between devices with their start and end apart: 5, of which 5 were waited for; matrix products, arithmetic and copies ran while one was open for 5% of the time, Pallas kernels for 0%

profile of v1, /device:TPU:0, one launch (start us, length us, event | category | flops | bytes accessed | tf_op | source)
XLA Modules:
  0.0 433.9 jit_solution(728283697706798864)
XLA Ops:
  5.1 12.6 %gather_fusion = s32[2048]{0:T(1024)S(1)} fusion(s32[16]{0:T(128)S(1)} %dynamic-slice_subtract_fusion, s32[2048]{0:T(1024)S(1)} %broadcast_clamp_fusion.2), kind=kCustom, calls=%fused_computation.4 | custom fusion | bytes 24576 | tf_op jit(solution)/shard_map/jit(_take)/gather | solution.py:96
  17.8 11.8 %gather_fusion.1 = s32[2048]{0:T(1024)S(1)} fusion(s32[4096]{0:T(1024)S(1)} %bitcast.42, s32[2048]{0:T(1024)S(1)} %broadcast_clamp_fusion.1), kind=kCustom, calls=%fused_computation.5 | custom fusion | bytes 24576 | tf_op jit(solution)/shard_map/jit(_take)/gather | solution.py:97
  30.4 7.5 %gather_fusion.4 = bf16[2048,256]{1,0:T(8,128)(2,1)S(1)} fusion(bf16[4096,256]{1,0:T(8,128)(2,1)S(1)} %bitcast.41, s32[2048]{0:T(1024)S(1)} %broadcast_clamp_fusion), kind=kCustom, calls=%fused_computation.2.clone | custom fusion | bytes 2105344 | tf_op jit(solution)/shard_map/jit(_take)/gather | solution.py:101
  37.9 10.3 %gather_fusion.2 = bf16[2048,256]{1,0:T(8,128)(2,1)} fusion(bf16[4096,256]{1,0:T(8,128)(2,1)} %bitcast.44, s32[2048]{0:T(1024)S(1)} %broadcast_clamp_fusion), kind=kCustom, calls=%fused_computation.clone | custom fusion | bytes 2105344 | tf_op jit(solution)/shard_map/jit(_take)/gather | solution.py:100
  48.2 3.7 select_select_fusion
  51.9 4.3 all-to-all-start.1
  56.2 5.1 %fusion.3 = f32[16384]{0:T(1024)S(1)} fusion(bf16[256,16384]{1,0:T(8,128)(2,1)} %param.14), kind=kLoop, calls=%fused_computation.17 | loop fusion | flops 12566528 | bytes 8454144 | tf_op jit(solution)/shard_map/reduce_sum | solution.py:14
  62.1 2.5 fusion.32
  64.7 5.1 %fusion.1 = f32[16384]{0:T(1024)S(1)} fusion(bf16[256,16384]{1,0:T(8,128)(2,1)} %param.13), kind=kLoop, calls=%fused_computation.15 | loop fusion | flops 12566528 | bytes 8454144 | tf_op jit(solution)/shard_map/reduce_sum | solution.py:14
  70.6 4.4 %all-to-all-start = ((bf16[4,512,256]{2,1,0:T(8,128)(2,1)}), bf16[4,512,256]{2,1,0:T(8,128)(2,1)}, u32[]{:S(2)}, u32[]{:S(2)}) async-start(bf16[4,512,256]{2,1,0:T(8,128)(2,1)} %get-tuple-element.25), calls=%async_computation | async-start | bytes 2097152 | tf_op jit(solution)/shard_map/all_to_all | solution.py:103
  75.1 5.4 %gather_fusion.5 = bf16[1536,256]{1,0:T(8,128)(2,1)} fusion(bf16[2048,256]{1,0:T(8,128)(2,1)S(1)} %bitcast.43, s32[2048]{0:T(1024)S(1)} %pad_clamp_fusion), kind=kCustom, calls=%fused_computation.3.clone | custom fusion | bytes 1579008 | tf_op jit(solution)/shard_map/jit(_take)/gather | solution.py:109
  80.5 1.6 fusion.7
  82.1 7.2 %all-to-all-done = bf16[4,512,256]{2,1,0:T(8,128)(2,1)} async-done(((bf16[4,512,256]{2,1,0:T(8,128)(2,1)}), bf16[4,512,256]{2,1,0:T(8,128)(2,1)}, u32[]{:S(2)}, u32[]{:S(2)}) %all-to-all-start) | async-done | bytes 1048608 | tf_op jit(solution)/shard_map/all_to_all | solution.py:103
  89.4 5.8 %gather_fusion.3 = bf16[1536,256]{1,0:T(8,128)(2,1)} fusion(bf16[2048,256]{1,0:T(8,128)(2,1)} %bitcast.10, s32[2048]{0:T(1024)S(1)} %pad_clamp_fusion), kind=kCustom, calls=%fused_computation.1.clone | custom fusion | bytes 1579008 | tf_op jit(solution)/shard_map/jit(_take)/gather | solution.py:106
  95.2 1.4 copy.16
  97.5 39.0 %multiply_exponential_fusion = f32[1536,16384]{1,0:T(8,128)} fusion(f32[16384]{0:T(1024)S(1)} %copy-done.10, bf16[256,16384]{1,0:T(8,128)(2,1)} %param.14, f32[16384]{0:T(1024)S(1)} %add_sqrt_fusion, f32[1536]{0:T(1024)S(1)} %add_sqrt_fusion.2, bf16[1536,256]{1,0:T(8,128)(2,1)} %gather_fusion.5, pred[1536]{0:T(1024)(128)(4,1)S(1)} %get-tuple-element.16), kind=kOutput, calls=%fused_computation.8 | convolution fusion | flops 12949389312 | bytes 109977088 | tf_op jit(solution)/shard_map/dot_general | solution.py:34
  136.5 69.8 %exponential_reduce_fusion = (f32[1536]{0:T(1024)S(1)}, f32[1536]{0:T(1024)S(1)}, f32[1536]{0:T(1024)S(1)}, f32[1536,16384]{1,0:T(8,128)}) fusion(f32[1536,16384]{1,0:T(8,128)} %multiply_exponential_fusion, bf16[256,16384]{1,0:T(8,128)(2,1)} %param.13, f32[16384]{0:T(1024)S(1)} %add_sqrt_fusion.1, f32[1536]{0:T(1024)S(1)} %get-tuple-element.23, ...), kind=kOutput, calls=%fused_computation.9 | convolution fusion | flops 13024880640 | bytes 210593280 | tf_op jit(solution)/shard_map/dot_general | solution.py:33
  206.3 38.1 %all-reduce = (f32[1536]{0:T(1024)}, f32[1536]{0:T(1024)S(1)}, f32[1536]{0:T(1024)S(1)}) all-reduce(f32[1536]{0:T(1024)S(1)} %get-tuple-element.11, f32[1536]{0:T(1024)S(1)} %get-tuple-element.12, f32[1536]{0:T(1024)S(1)} %get-tuple-element.10), channel_id=1, replica_groups=mesh['dp'=4,'proto'=8] {'proto'}, use_global_device_ids=true, to_apply=%region_14.17 | all-reduce | flops 4608 | bytes 36864 | tf_op jit(solution)/shard_map/psum | solution.py:37
  244.4 67.5 %fusion = f32[1536,256]{0,1:T(8,128)} fusion(f32[1536,16384]{1,0:T(8,128)} %multiply_exponential_fusion, f32[1536,16384]{1,0:T(8,128)} %get-tuple-element.32, f32[1536]{0:T(1024)S(1)} %get-tuple-element.14, f32[1536]{0:T(1024)S(1)} %get-tuple-element.15, bf16[256,16384]{1,0:T(8,128)(2,1)} %param.13, f32[16384]{0:T(1024)S(1)} %add_sqrt_fusion.1), kind=kOutput, calls=%fused_computation.10 | convolution fusion | flops 13048479744 | bytes 211365888 | tf_op jit(solution)/shard_map/dot_general | solution.py:50
  312.0 28.8 %collective-permute-done = f32[1536,256]{0,1:T(8,128)S(1)} collective-permute-done((f32[1536,256]{0,1:T(8,128)}, f32[1536,256]{0,1:T(8,128)S(1)}, u32[]{:S(2)}, u32[]{:S(2)}) %collective-permute-start) | collective-permute-done | bytes 1572896 | tf_op jit(solution)/shard_map/ppermute | solution.py:55
  340.8 1.7 add.245
  342.5 32.1 %collective-permute-done.1 = f32[1536,256]{0,1:T(8,128)S(1)} collective-permute-done((f32[1536,256]{0,1:T(8,128)S(1)}, f32[1536,256]{0,1:T(8,128)S(1)}, u32[]{:S(2)}, u32[]{:S(2)}) %collective-permute-start.1) | collective-permute-done | bytes 1572896 | tf_op jit(solution)/shard_map/ppermute | solution.py:55
  375.5 56.4 %collective-permute-done.2 = f32[1536,256]{0,1:T(8,128)S(1)} collective-permute-done((f32[1536,256]{0,1:T(8,128)S(1)}, f32[1536,256]{0,1:T(8,128)S(1)}, u32[]{:S(2)}, u32[]{:S(2)}) %collective-permute-start.2) | collective-permute-done | bytes 1572896 | tf_op jit(solution)/shard_map/ppermute | solution.py:55
  432.8 1.2 copy.17
  (67 shorter events, 9.7 us)
Async XLA Ops:
  0.6 29.8 %copy-start = (bf16[16,256,256]{2,1,0:T(8,128)(2,1)S(1)}, bf16[16,256,256]{2,1,0:T(8,128)(2,1)}, u32[]{:S(2)}) copy-start(bf16[16,256,256]{2,1,0:T(8,128)(2,1)} %param.12) | copy-start | bytes 6291460
  0.6 17.1 %copy-start.8 = (s32[16,256]{1,0:T(8,128)S(1)}, s32[16,256]{1,0:T(8,128)}, u32[]{:S(2)}) copy-start(s32[16,256]{1,0:T(8,128)} %param.17) | copy-start | bytes 49156
  51.9 18.7 %all-to-all-start.1 = ((bf16[4,512,256]{2,1,0:T(8,128)(2,1)}), bf16[4,512,256]{2,1,0:T(8,128)(2,1)S(1)}, u32[]{:S(2)}, u32[]{:S(2)}) async-start(bf16[4,512,256]{2,1,0:T(8,128)(2,1)} %get-tuple-element.24), calls=%async_computation.1 | async-start | bytes 2097152 | tf_op jit(solution)/shard_map/all_to_all | solution.py:104
  64.7 71.9 %copy-start.5 = (pred[1536]{0:T(1024)(128)(4,1)}, pred[1536]{0:T(1024)(128)(4,1)S(1)}, u32[]{:S(2)}) copy-start(pred[1536]{0:T(1024)(128)(4,1)S(1)} %get-tuple-element.16) | copy-start | bytes 4612
  70.6 18.8 %all-to-all-start = ((bf16[4,512,256]{2,1,0:T(8,128)(2,1)}), bf16[4,512,256]{2,1,0:T(8,128)(2,1)}, u32[]{:S(2)}, u32[]{:S(2)}) async-start(bf16[4,512,256]{2,1,0:T(8,128)(2,1)} %get-tuple-element.25), calls=%async_computation | async-start | bytes 2097152 | tf_op jit(solution)/shard_map/all_to_all | solution.py:103
  75.1 22.4 %copy-start.10 = (f32[16384]{0:T(1024)S(1)}, f32[16384]{0:T(1024)}, u32[]{:S(2)}) copy-start(f32[16384]{0:T(1024)} %param.15) | copy-start | bytes 196612
  96.6 39.9 %copy-start.1 = (bf16[1536,256]{0,1:T(8,128)(2,1)}, bf16[1536,256]{0,1:T(8,128)(2,1)S(1)}, u32[]{:S(2)}) copy-start(bf16[1536,256]{0,1:T(8,128)(2,1)S(1)} %copy.16) | copy-start | bytes 2359300
  97.5 39.0 %copy-start.3 = (f32[1536]{0:T(1024)}, f32[1536]{0:T(1024)S(1)}, u32[]{:S(2)}) copy-start(f32[1536]{0:T(1024)S(1)} %get-tuple-element.23) | copy-start | bytes 18436
  311.9 63.0 %copy-start.9 = (f32[1536]{0:T(1024)S(1)}, f32[1536]{0:T(1024)}, u32[]{:S(2)}) copy-start(f32[1536]{0:T(1024)} %get-tuple-element.13) | copy-start | bytes 18436
  311.9 120.0 %copy-start.2 = (bf16[1536,256]{0,1:T(8,128)(2,1)S(1)}, bf16[1536,256]{0,1:T(8,128)(2,1)}, u32[]{:S(2)}) copy-start(bf16[1536,256]{0,1:T(8,128)(2,1)} %copy-done.1) | copy-start | bytes 2359300
  311.9 120.0 %copy-start.6 = (pred[1536]{0:T(1024)(128)(4,1)S(1)}, pred[1536]{0:T(1024)(128)(4,1)}, u32[]{:S(2)}) copy-start(pred[1536]{0:T(1024)(128)(4,1)} %copy-done.5) | copy-start | bytes 4612
  311.9 120.4 %copy-start.4 = (f32[1536]{0:T(1024)S(1)}, f32[1536]{0:T(1024)}, u32[]{:S(2)}) copy-start(f32[1536]{0:T(1024)} %copy-done.3) | copy-start | bytes 18436
  311.9 120.4 %copy-start.7 = (f32[1536]{0:T(1024)S(1)}, f32[1536]{0:T(1024)}, u32[]{:S(2)}) copy-start(f32[1536]{0:T(1024)} %get-tuple-element.22) | copy-start | bytes 18436
  311.9 28.8 %collective-permute-start = (f32[1536,256]{0,1:T(8,128)}, f32[1536,256]{0,1:T(8,128)S(1)}, u32[]{:S(2)}, u32[]{:S(2)}) collective-permute-start(f32[1536,256]{0,1:T(8,128)} %fusion), channel_id=1, source_target_pairs={{0,1},{1,0},{2,3},{3,2},{4,5},{5,4},{6,7},{7,6},{8,9},{9,8},{10,11... | collective-permute-start | bytes 4718600 | tf_op jit(solution)/shard_map/ppermute | solution.py:55
  342.4 32.2 %collective-permute-start.1 = (f32[1536,256]{0,1:T(8,128)S(1)}, f32[1536,256]{0,1:T(8,128)S(1)}, u32[]{:S(2)}, u32[]{:S(2)}) collective-permute-start(f32[1536,256]{0,1:T(8,128)S(1)} %add.245), channel_id=1, source_target_pairs={{0,2},{1,3},{2,0},{3,1},{4,6},{5,7},{6,4},{7,5},{8,10},{9,11},{10,... | collective-permute-start | bytes 4718600 | tf_op jit(solution)/shard_map/ppermute | solution.py:55
  374.8 57.1 %collective-permute-start.2 = (f32[1536,256]{0,1:T(8,128)S(1)}, f32[1536,256]{0,1:T(8,128)S(1)}, u32[]{:S(2)}, u32[]{:S(2)}) collective-permute-start(f32[1536,256]{0,1:T(8,128)S(1)} %add.246), channel_id=1, source_target_pairs={{0,4},{1,5},{2,6},{3,7},{4,0},{5,1},{6,2},{7,3},{8,12},{9,13},{10,... | collective-permute-start | bytes 4718600 | tf_op jit(solution)/shard_map/ppermute | solution.py:55
